TPU v7x, 256 devices: a whole 4x4x8 slice. The times are simulated.
256 devices in a mesh: group: 32 (over x, y, core), tp: 8 (over z).
Axes of the slice: x: 4, y: 4, z: 8, core: 2. Of those that a mesh axis runs over, the one named last changes fastest.
Arguments:
- hidden_in: bfloat16 [64, 3072], P('group'), may hold values from -6 to 6
- w_qkv: bfloat16 [3072, 2048], P(None, 'tp'), may hold values from -0.109375 to 0.109375
- w_out: bfloat16 [1536, 3072], P('tp'), may hold values from -0.15625 to 0.15625
- kv_pool: bfloat16 [2048, 128, 512], P(('group', 'tp'))
- page_table: int32 [64, 32], replicated, may hold values from 0 to 2047, as said below
- lengths: int32 [64], replicated, may hold values from 1 to 4096, as said below
Outputs:
- attn_proj: bfloat16 [64, 3072], P('group', 'tp')
Inputs may be any that keep to these rules, and one draw needn't show every extreme that they name: `page_table`: every pool slot is named by exactly one request page. `lengths`: some request has the full 32 * 128 cached tokens.
All inputs are finite; a program needn't handle non-finite values.
Results may differ from a plain program's by a relative error of at most 0.0085.
The roundings to bfloat16 on the way count: a program that leaves them out, or rounds other values in their place, can miss the bound.
Values may be sent and summed in bfloat16 or wider, within the bound.
A program may use at most 64 MiB of HBM per device.

v0:
```python
import jax
import jax.numpy as jnp
from jax import lax
from jax.sharding import PartitionSpec as P

HEADS = 12
KV_HEADS = 2
HEAD_DIM = 128


def on_device(hidden_in, w_qkv, w_out, kv_pool, page_table, lengths):
    qdim = HEADS * HEAD_DIM
    kdim = KV_HEADS * HEAD_DIM
    per_kv = HEADS // KV_HEADS
    scale = HEAD_DIM ** (-0.5)
    req_grp = hidden_in.shape[0]
    col_count = w_out.shape[0]
    col_start = lax.axis_index("tp") * col_count
    columns = jnp.dot(hidden_in, w_qkv, preferred_element_type=jnp.float32).astype(jnp.bfloat16)
    qkv = lax.all_gather(columns, "tp", axis=1, tiled=True)
    queries = lax.all_gather(qkv[:, :qdim], "group", axis=0, tiled=True)
    requests = queries.shape[0]
    slot_count = kv_pool.shape[0]
    page_len = kv_pool.shape[1]
    max_pages = page_table.shape[1]
    slot_ids = lax.axis_index(("group", "tp")) * slot_count + jnp.arange(
        slot_count, dtype=jnp.int32
    )
    match = page_table[:, :, None] == slot_ids[None, None, :]
    slot_req = jnp.sum(
        jnp.where(match, jnp.arange(requests, dtype=jnp.int32)[:, None, None], 0), axis=(0, 1)
    )
    slot_page = jnp.sum(
        jnp.where(match, jnp.arange(max_pages, dtype=jnp.int32)[None, :, None], 0), axis=(0, 1)
    )
    chosen = queries[slot_req].reshape(slot_count, KV_HEADS, per_kv, HEAD_DIM)
    keys = kv_pool[..., :kdim].reshape(slot_count, page_len, KV_HEADS, HEAD_DIM)
    values = kv_pool[..., kdim:].reshape(slot_count, page_len, KV_HEADS, HEAD_DIM)
    scores = jnp.einsum("pgjd,ptgd->pgjt", chosen, keys, preferred_element_type=jnp.float32) * scale
    position = slot_page[:, None] * page_len + jnp.arange(page_len, dtype=jnp.int32)[None, :]
    live = (position < lengths[slot_req][:, None])[:, None, None, :]
    top = jnp.max(jnp.where(live, scores, -1e30), axis=-1)
    probs = jnp.where(live, jnp.exp(scores - top[..., None]), 0.0).astype(jnp.bfloat16)
    total = jnp.sum(probs.astype(jnp.float32), axis=-1)
    weighted = jnp.einsum("pgjt,ptgd->pgjd", probs, values, preferred_element_type=jnp.float32)
    owner = slot_req[None, :] == jnp.arange(requests, dtype=jnp.int32)[:, None]
    req_top = jnp.max(jnp.where(owner[:, :, None, None], top[None], -1e30), axis=1)
    factor = jnp.exp(top - req_top[slot_req])
    onehot = owner.astype(jnp.float32)
    req_total = jnp.einsum(
        "rp,pgj->rgj", onehot, total * factor, precision=lax.Precision.HIGHEST
    ).reshape(requests, HEADS)
    req_sums = jnp.einsum(
        "rp,pgjd->rgjd", onehot, weighted * factor[..., None], precision=lax.Precision.HIGHEST
    ).reshape(requests, qdim)
    req_top = req_top.reshape(requests, HEADS)
    start = lax.axis_index("group") * req_grp
    peak_all = lax.pmax(req_top, ("group", "tp"))
    rescale = jnp.exp(req_top - peak_all)
    total_all, sums_all = lax.psum(
        (req_total * rescale, req_sums * jnp.repeat(rescale, HEAD_DIM, axis=1)), ("group", "tp")
    )
    peak = lax.dynamic_slice_in_dim(peak_all, start, req_grp, 0)
    whole = lax.dynamic_slice_in_dim(total_all, start, req_grp, 0)
    sums = lax.dynamic_slice_in_dim(sums_all, start, req_grp, 0)
    sums_part = lax.dynamic_slice_in_dim(sums, col_start, col_count, 1)
    own_q = qkv[:, :qdim].reshape(req_grp, KV_HEADS, per_kv, HEAD_DIM)
    own_k = qkv[:, qdim : qdim + kdim].reshape(req_grp, KV_HEADS, HEAD_DIM)
    own_v = qkv[:, qdim + kdim :].reshape(req_grp, KV_HEADS, HEAD_DIM)
    own_score = (
        jnp.einsum("rgjd,rgd->rgj", own_q, own_k, preferred_element_type=jnp.float32) * scale
    ).reshape(req_grp, HEADS)
    own_sums = jnp.broadcast_to(
        own_v.astype(jnp.float32)[:, :, None, :], (req_grp, KV_HEADS, per_kv, HEAD_DIM)
    ).reshape(req_grp, qdim)
    new_peak = jnp.maximum(peak, own_score)
    old_factor = jnp.exp(peak - new_peak)
    own_factor = jnp.exp(own_score - new_peak)
    new_whole = whole * old_factor + own_factor

    def pick(values_full):
        return lax.dynamic_slice_in_dim(values_full, col_start, col_count, 1)

    new_sums = sums_part * pick(jnp.repeat(old_factor, HEAD_DIM, axis=1)) + pick(
        own_sums * jnp.repeat(own_factor, HEAD_DIM, axis=1)
    )
    attn_part = (new_sums / pick(jnp.repeat(new_whole, HEAD_DIM, axis=1))).astype(jnp.bfloat16)
    partial_value = jnp.dot(attn_part, w_out, preferred_element_type=jnp.float32)
    return lax.psum_scatter(partial_value, "tp", scatter_dimension=1, tiled=True).astype(
        jnp.bfloat16
    )


def solution(mesh):
    in_specs = (
        P("group", None),
        P(None, "tp"),
        P("tp", None),
        P(("group", "tp"), None, None),
        P(),
        P(),
    )
    out_specs = P("group", "tp")
    return jax.shard_map(
        on_device, mesh=mesh, in_specs=in_specs, out_specs=out_specs, check_vma=False
    )
```

profile of v0, /device:TPU:2, one launch (start us, length us, event | category | flops | bytes accessed | tf_op | source)
XLA Modules:
  0.0 429.0 jit_solution(9588263399593622062)
XLA Ops:
  6.5 1.1 fusion.1
  7.7 0.2 copy-done
  8.0 1.0 convolution_convert_fusion
  9.0 19.1 %all_gather.6 = bf16[2,2048]{1,0:T(2,128)(2,1)S(1)} all-gather(bf16[2,256]{1,0:T(2,128)(2,1)S(1)} %convolution_convert_fusion), channel_id=1, replica_groups=mesh['group'=32,'tp'=8] {'tp'}, dimensions={1}, use_global_device_ids=true | all-gather | bytes 9216 | tf_op jit(solution)/shard_map/all_gather | solution.py:20
  28.1 24.7 %all-gather = bf16[32,2,1536]{2,1,0:T(2,128)(2,1)S(1)} all-gather(bf16[1,2,1536]{2,1,0:T(2,128)(2,1)S(1)} %get-tuple-element.19), channel_id=1, replica_groups=mesh['group'=32,'tp'=8] {'group'}, dimensions={0}, use_global_device_ids=true | all-gather | bytes 202752 | tf_op jit(solution)/shard_map/all_gather | solution.py:21
  52.9 0.6 gather_fusion
  53.5 0.6 gather_fusion.1
  54.1 1.3 fusion.25
  55.4 0.3 copy.96
  55.8 0.3 select_reduce_fusion
  56.4 0.3 copy.97
  56.7 0.2 convert_reduce_fusion
  57.0 74.0 %pmax.7 = f32[64,12]{1,0:T(8,128)S(1)} all-reduce(f32[64,12]{1,0:T(8,128)S(1)} %copy.86), channel_id=1, replica_groups=mesh['group'=32,'tp'=8] {'group','tp'}, use_global_device_ids=true, to_apply=%region_4.5 | all-reduce | flops 768 | bytes 6144 | tf_op jit(solution)/shard_map/pmax | solution.py:58
  131.0 0.6 gather_fusion.2
  131.9 0.4 convolution_multiply_fusion
  132.3 0.4 fusion.2
  132.8 0.2 copy.84
  133.2 0.2 broadcast_in_dim.104
  133.4 0.9 bitcast_multiply_fusion
  134.6 74.9 %psum.15 = f32[64,12]{1,0:T(8,128)S(1)} all-reduce(f32[64,12]{1,0:T(8,128)S(1)} %get-tuple-element.10), channel_id=1, replica_groups=mesh['group'=32,'tp'=8] {'group','tp'}, use_global_device_ids=true, to_apply=%region_7.8 | all-reduce | flops 768 | bytes 6144 | tf_op jit(solution)/shard_map/psum | solution.py:60
  209.7 168.6 %all-reduce.2.cloned.1.call-done = f32[64,1536]{1,0:T(8,128)} async-done(((f32[64,1536]{1,0:T(8,128)}), f32[64,1536]{1,0:T(8,128)}) %all-reduce.2.cloned.1.call-update) | async-done | bytes 393232 | tf_op jit(solution)/shard_map/psum | solution.py:60
  378.3 2.7 convolution_bitcast_fusion
  381.0 39.5 %reduce-scatter.4.cloned.1.call-done = f32[384,2]{1,0:T(8,128)} async-done(((f32[3072,2]{1,0:T(8,128)}), f32[384,2]{1,0:T(8,128)}) %reduce-scatter.4.cloned.1.call-update) | async-done | bytes 3088
  420.5 1.6 copy.95
  (43 shorter events, 1.6 us)
Async XLA Ops:
  6.5 1.4 copy-start
  6.5 46.4 %copy-start.1 = (s32[64]{0:T(128)S(1)}, s32[64]{0:T(128)}, u32[]{:S(2)}) copy-start(s32[64]{0:T(128)} %param.11) | copy-start | bytes 772
  6.5 371.7 %all-reduce.2.cloned.1.call-start = ((), (), s32[]{:S(2)}) async-start(), calls=%async_computation.1 | async-start | bytes 786432 | tf_op jit(solution)/shard_map/psum | solution.py:60
  133.1 245.2 %copy-start.2 = (bf16[192,3072]{1,0:T(8,128)(2,1)S(1)}, bf16[192,3072]{1,0:T(8,128)(2,1)}, u32[]{:S(2)}) copy-start(bf16[192,3072]{1,0:T(8,128)(2,1)} %param.8) | copy-start | bytes 3538948
  134.3 286.2 %reduce-scatter.4.cloned.1.call-start = ((), (), s32[]{:S(2)}) async-start(), calls=%async_computation.2 | async-start | bytes 1769472
Sparse Core Ops, SparseCore 0:
  134.4 243.8 all-reduce.1
  381.1 39.3 reduce-scatter.3
where the time goes:
time: 430 us; the launch traced here: 429 us
  waiting for transfers between devices  208 us (48%)
  blocking collectives  193 us (45%)
  between operations  13.6 us (3%)
  local copies, waits for them, and re-layouts  6.81 us (2%)
  matrix products  5.21 us (1%)
    psum x1, waiting for transfers between devices, on_device(): lax.psum((req_total * rescale, req_sums * jnp.repeat(rescale, HEAD_DIM, a...  169 us
    psum x1, blocking collectives, on_device(): lax.psum((req_total * rescale, req_sums * jnp.repeat(rescale, HEAD_DIM, a...  74.9 us
    pmax x1, blocking collectives, on_device(): peak_all = lax.pmax(req_top, ('group', 'tp'))  74 us
    unnamed x3, waiting for transfers between devices  39.6 us
    all_gather x1, blocking collectives, on_device(): queries = lax.all_gather(qkv[:, :qdim], 'group', axis=0, tiled=True)  24.7 us
    all_gather x1, blocking collectives, on_device(): qkv = lax.all_gather(columns, 'tp', axis=1, tiled=True)  19.1 us
  transfers between devices with their start and end apart: 2, of which 2 were waited for; matrix products, arithmetic and copies ran while one was open for 0% of the time, Pallas kernels for 0%

commit v1 on v0

--- a/solution.py
+++ b/solution.py
@@ -6,6 +6,12 @@
 HEADS = 12
 KV_HEADS = 2
 HEAD_DIM = 128
+
+
+def laid_out(parts, dim):
+    parts = jnp.moveaxis(parts, 0, dim)
+    shape = parts.shape
+    return parts.reshape(*shape[:dim], shape[dim] * shape[dim + 1], *shape[dim + 2 :])
 
 
 def on_device(hidden_in, w_qkv, w_out, kv_pool, page_table, lengths):
@@ -17,7 +23,19 @@
     col_count = w_out.shape[0]
     col_start = lax.axis_index("tp") * col_count
     columns = jnp.dot(hidden_in, w_qkv, preferred_element_type=jnp.float32).astype(jnp.bfloat16)
-    qkv = lax.all_gather(columns, "tp", axis=1, tiled=True)
+    devices = lax.axis_size("tp")
+    pairs = [(i, (i + 1) % devices) for i in range(devices)]
+    back = [(b, a) for a, b in pairs]
+    lower, upper = ([], [])
+    for step in range(devices - 1):
+        if step % 2 == 0:
+            lower.append(lax.ppermute(lower[-1] if lower else columns, "tp", pairs))
+        else:
+            upper.append(lax.ppermute(upper[-1] if upper else columns, "tp", back))
+    parts = jnp.stack([*lower[::-1], columns, *upper])
+    shift = lax.axis_index("tp") - len(lower)
+    parts = parts[(jnp.arange(devices) - shift) % devices]
+    qkv = laid_out(parts, 1)
     queries = lax.all_gather(qkv[:, :qdim], "group", axis=0, tiled=True)
     requests = queries.shape[0]
     slot_count = kv_pool.shape[0]

time: 430 us -> 510 us (1.19)
  waiting for transfers between devices: 208 us -> 293 us
  blocking collectives: 193 us -> 175 us
  starting transfers between devices: 0.04 us -> 12.5 us
    psum x1, waiting for transfers between devices: 169 us -> 244 us  [on_device(): lax.psum((req_total * rescale, req_sums * jnp.repeat(rescale, HEAD_DIM, a...]
    all_gather x1 -> x0, blocking collectives: 19.1 us -> none  [on_device(): qkv = lax.all_gather(columns, 'tp', axis=1, tiled=True)]
    ppermute x0 -> x7, starting transfers between devices: none -> 12.5 us  [the longest x3 12.5 us: on_device(): upper.append(lax.ppermute(upper[-1] if upper else columns, 'tp', back))]
    ppermute x0 -> x7, waiting for transfers between devices: none -> 9.88 us  [the longest x4 9.54 us: on_device(): lower.append(lax.ppermute(lower[-1] if lower else columns, 'tp', pairs))]
  transfers between devices with their start and end apart: 2 -> 9, of which waited for: 2 -> 7; matrix products, arithmetic and copies ran while one was open for 0% -> 1% of each run, Pallas kernels for 0% -> 0%
where the time goes in v1:
time: 510 us; the launch traced here: 509 us
  waiting for transfers between devices  293 us (57%)
  blocking collectives  175 us (34%)
  between operations  13.6 us (3%)
  starting transfers between devices  12.5 us (2%)
  local copies, waits for them, and re-layouts  8.62 us (2%)
  matrix products  5.19 us (1%)
    psum x1, waiting for transfers between devices, on_device(): lax.psum((req_total * rescale, req_sums * jnp.repeat(rescale, HEAD_DIM, a...  244 us
    pmax x1, blocking collectives, on_device(): peak_all = lax.pmax(req_top, ('group', 'tp'))  76.4 us
    psum x1, blocking collectives, on_device(): lax.psum((req_total * rescale, req_sums * jnp.repeat(rescale, HEAD_DIM, a...  73.5 us
    unnamed x3, waiting for transfers between devices  39.6 us
    all_gather x1, blocking collectives, on_device(): queries = lax.all_gather(qkv[:, :qdim], 'group', axis=0, tiled=True)  24.7 us
    ppermute x3, starting transfers between devices, on_device(): upper.append(lax.ppermute(upper[-1] if upper else columns, 'tp', back))  12.5 us
  transfers between devices with their start and end apart: 9, of which 7 were waited for; matrix products, arithmetic and copies ran while one was open for 1% of the time, Pallas kernels for 0%

profile of v1, /device:TPU:2, one launch (start us, length us, event | category | flops | bytes accessed | tf_op | source)
XLA Modules:
  0.0 509.3 jit_solution(17270678631975801813)
XLA Ops:
  6.5 1.4 copy-done
  7.9 1.0 convolution_convert_fusion
  9.0 5.9 %collective-permute-start.4 = (bf16[2,256]{1,0:T(2,128)(2,1)S(1)}, bf16[2,256]{1,0:T(2,128)(2,1)S(1)}, u32[]{:S(2)}, u32[]{:S(2)}) collective-permute-start(bf16[2,256]{1,0:T(2,128)(2,1)S(1)} %convolution_convert_fusion), channel_id=1, source_target_pairs={{1,0},{2,1},{3,2},{4,3},{5,4},{6,5},{7,6},{0,7},{9,8},{10,9},{11,1... | collective-permute-start | bytes 3080 | tf_op jit(solution)/shard_map/ppermute | solution.py:34
  15.1 1.3 fusion.27
  16.4 0.6 gather_fusion
  17.2 2.4 collective-permute-done
  19.6 4.8 collective-permute-done.1
  24.4 3.3 collective-permute-start.5
  27.7 1.5 collective-permute-done.2
  29.7 3.3 collective-permute-start.6
  33.0 0.9 collective-permute-done.3
  34.4 0.6 gather_fusion.1
  35.0 24.7 %all-gather = bf16[32,2,1536]{2,1,0:T(2,128)(2,1)S(1)} all-gather(bf16[1,2,1536]{2,1,0:T(2,128)(2,1)S(1)} %get-tuple-element.19), channel_id=1, replica_groups=mesh['group'=32,'tp'=8] {'group'}, dimensions={0}, use_global_device_ids=true | all-gather | bytes 202752 | tf_op jit(solution)/shard_map/all_gather | solution.py:39
  59.7 0.6 gather_fusion.2
  61.5 76.4 %pmax.7 = f32[64,12]{1,0:T(8,128)S(1)} all-reduce(f32[64,12]{1,0:T(8,128)S(1)} %copy.86), channel_id=1, replica_groups=mesh['group'=32,'tp'=8] {'group','tp'}, use_global_device_ids=true, to_apply=%region_4.5 | all-reduce | flops 768 | bytes 6144 | tf_op jit(solution)/shard_map/pmax | solution.py:76
  137.9 0.6 gather_fusion.3
  138.8 73.5 %psum.15 = f32[64,12]{1,0:T(8,128)S(1)} all-reduce(f32[64,12]{1,0:T(8,128)S(1)} %get-tuple-element.10), channel_id=1, replica_groups=mesh['group'=32,'tp'=8] {'group','tp'}, use_global_device_ids=true, to_apply=%region_7.8 | all-reduce | flops 768 | bytes 6144 | tf_op jit(solution)/shard_map/psum | solution.py:78
  212.5 0.4 convolution_multiply_fusion
  212.9 0.4 fusion.2
  213.9 0.9 bitcast_multiply_fusion
  215.0 243.7 %all-reduce.2.cloned.1.call-done = f32[64,1536]{1,0:T(8,128)} async-done(((f32[64,1536]{1,0:T(8,128)}), f32[64,1536]{1,0:T(8,128)}) %all-reduce.2.cloned.1.call-update) | async-done | bytes 393232 | tf_op jit(solution)/shard_map/psum | solution.py:78
  458.6 2.7 convolution_bitcast_fusion
  461.3 39.5 %reduce-scatter.4.cloned.1.call-done = f32[384,2]{1,0:T(8,128)} async-done(((f32[3072,2]{1,0:T(8,128)}), f32[384,2]{1,0:T(8,128)}) %reduce-scatter.4.cloned.1.call-update) | async-done | bytes 3088
  500.9 1.6 copy.95
  (69 shorter events, 3.8 us)
Async XLA Ops:
  6.5 1.4 copy-start
  6.5 8.3 %copy-start.3 = (s32[64,32]{0,1:T(8,128)S(1)}, s32[64,32]{0,1:T(8,128)}, u32[]{:S(2)}) copy-start(s32[64,32]{0,1:T(8,128)} %param.10) | copy-start | bytes 24580
  6.5 9.8 %copy-start.1 = (s32[64]{0:T(128)S(1)}, s32[64]{0:T(128)}, u32[]{:S(2)}) copy-start(s32[64]{0:T(128)} %param.11) | copy-start | bytes 772
  6.5 452.1 %all-reduce.2.cloned.1.call-start = ((), (), s32[]{:S(2)}) async-start(), calls=%async_computation.1 | async-start | bytes 786432 | tf_op jit(solution)/shard_map/psum | solution.py:78
  9.0 15.4 %collective-permute-start.4 = (bf16[2,256]{1,0:T(2,128)(2,1)S(1)}, bf16[2,256]{1,0:T(2,128)(2,1)S(1)}, u32[]{:S(2)}, u32[]{:S(2)}) collective-permute-start(bf16[2,256]{1,0:T(2,128)(2,1)S(1)} %convolution_convert_fusion), channel_id=1, source_target_pairs={{1,0},{2,1},{3,2},{4,3},{5,4},{6,5},{7,6},{0,7},{9,8},{10,9},{11,1... | collective-permute-start | bytes 3080 | tf_op jit(solution)/shard_map/ppermute | solution.py:34
  14.8 4.8 collective-permute-start
  19.6 4.8 collective-permute-start.1
  24.4 4.8 collective-permute-start.2
  24.4 5.3 %collective-permute-start.5 = (bf16[2,256]{1,0:T(2,128)(2,1)S(1)}, bf16[2,256]{1,0:T(2,128)(2,1)S(1)}, u32[]{:S(2)}, u32[]{:S(2)}) collective-permute-start(bf16[2,256]{1,0:T(2,128)(2,1)S(1)} %collective-permute-done.4), channel_id=1, source_target_pairs={{1,0},{2,1},{3,2},{4,3},{5,4},{6,5},{7,6},{0,7},{9,8},{10,9},{11,1... | collective-permute-start | bytes 3080 | tf_op jit(solution)/shard_map/ppermute | solution.py:34
  29.2 4.8 collective-permute-start.3
  29.7 4.6 collective-permute-start.6
  213.7 245.0 %copy-start.2 = (bf16[192,3072]{1,0:T(8,128)(2,1)S(1)}, bf16[192,3072]{1,0:T(8,128)(2,1)}, u32[]{:S(2)}) copy-start(bf16[192,3072]{1,0:T(8,128)(2,1)} %param.8) | copy-start | bytes 3538948
  214.8 286.1 %reduce-scatter.4.cloned.1.call-start = ((), (), s32[]{:S(2)}) async-start(), calls=%async_computation.2 | async-start | bytes 1769472
Sparse Core Ops, SparseCore 0:
  214.9 243.6 all-reduce.1
  461.5 39.3 reduce-scatter.3
